TPU v7x, 512 devices: a whole 4x4x16 slice. The times are simulated.
512 devices in a mesh: space: 32 (over z, x_lo), chan: 16 (over x_hi, y, core).
Axes of the slice: x: 4 (x_hi: 2, x_lo: 2; x = x_hi * 2 + x_lo), y: 4, z: 16, core: 2. Of those that a mesh axis runs over, the one named last changes fastest.
Arguments:
- volume: bfloat16 [64, 256, 8, 128], P('space', 'chan'), may hold values from -6 to 6
- kernel: bfloat16 [27, 256, 256], P(None, 'chan'), may hold values from -0.078125 to 0.078125
- cotangent: bfloat16 [64, 256, 8, 128], P('space', 'chan'), may hold values from -6 to 6
Outputs:
- output_map: bfloat16 [64, 256, 8, 128], P('space', 'chan')
- input_grad: bfloat16 [64, 256, 8, 128], P('space', 'chan')
- kernel_grad: float32 [27, 256, 256], P(None, 'chan')
All inputs are finite; a program needn't handle non-finite values.
Results may differ from a plain program's by a relative error of at most 0.001.
Values may be sent and summed in bfloat16 or wider, within the bound.
A program may use at most 128 MiB of HBM per device.

v0:
```python
import math
import jax
import jax.numpy as jnp
from jax import lax
from jax.sharding import PartitionSpec as P


def with_halo(block, sides, width):
    for axis, dim in sides:
        count = lax.axis_size(axis)
        forward = [(i, i + 1) for i in range(count - 1)]
        backward = [(target, source) for source, target in forward]
        low = lax.ppermute(
            lax.slice_in_dim(block, block.shape[dim] - width, None, axis=dim), axis, forward
        )
        high = lax.ppermute(lax.slice_in_dim(block, 0, width, axis=dim), axis, backward)
        block = jnp.concatenate([low, block, high], axis=dim)
    return block


def plane_stack(piece, height, width, flipped):
    cells = height * width
    padded = jnp.pad(piece, ((0, 0), (0, 0), (width + 1, width + 1)))
    column = lax.broadcasted_iota(jnp.int32, (1, 1, cells), 2) % width
    windows = []
    for row_step in range(3):
        for col_step in range(3):
            row_from = 2 - row_step if flipped else row_step
            col_from = 2 - col_step if flipped else col_step
            offset = width + 1 + (row_from - 1) * width + (col_from - 1)
            shifted = padded[:, :, offset : offset + cells]
            target = column + (col_from - 1)
            inside = ((target >= 0) & (target < width)).astype(piece.dtype)
            windows.append(shifted * inside)
    return jnp.concatenate(windows, axis=1)


def on_device(volume, kernel, cotangent):
    depth, chans_local, height, width = volume.shape
    filters_local = cotangent.shape[1]
    cells = height * width
    scale_factor = 1.0 / math.sqrt(depth * lax.axis_size("space") * height * width)
    volume_flat = volume.reshape(depth, chans_local, cells)
    grad_flat = cotangent.reshape(depth, filters_local, cells)
    columns = lax.all_to_all(kernel, "chan", split_axis=2, concat_axis=1, tiled=True)
    init_output = jnp.zeros((depth, filters_local, cells), jnp.float32)
    init_input = jnp.zeros((depth, chans_local, cells), jnp.float32)
    rims = with_halo(volume_flat, (("space", 0),), 1)
    piece = lax.all_gather(rims, "chan", axis=1, tiled=True)
    output_acc = init_output
    count = piece.shape[1]
    stacked = plane_stack(piece, height, width, False)
    grads = []
    for depth_step in range(3):
        window = stacked[depth_step : depth_step + depth]
        taps = kernel[9 * depth_step : 9 * depth_step + 9]
        weights = jnp.transpose(taps, (1, 0, 2)).reshape(filters_local, 9 * count)
        output_acc = output_acc + jnp.einsum(
            "fj,zjp->zfp", weights, window, preferred_element_type=jnp.float32
        )
        term = jnp.einsum("zfp,zjp->fj", grad_flat, window, preferred_element_type=jnp.float32)
        grads.append(jnp.transpose(term.reshape(filters_local, 9, count), (1, 0, 2)))
    kernel_acc = jnp.concatenate(grads, axis=0)
    output_acc, kernel_acc = (output_acc, kernel_acc)
    grad_ext = with_halo(grad_flat, (("space", 0),), 1)
    total = init_input
    piece = lax.all_gather(grad_ext, "chan", axis=1, tiled=True)
    count = piece.shape[1]
    stacked = plane_stack(piece, height, width, True)
    for depth_step in range(3):
        window = stacked[2 - depth_step : 2 - depth_step + depth]
        taps = columns[9 * depth_step : 9 * depth_step + 9]
        weights = jnp.transpose(taps, (2, 0, 1)).reshape(chans_local, 9 * count)
        total = total + jnp.einsum(
            "kj,zjp->zkp", weights, window, preferred_element_type=jnp.float32
        )
    kernel_grad = lax.psum(kernel_acc, "space") * scale_factor
    output_map = output_acc.astype(jnp.bfloat16).reshape(depth, filters_local, height, width)
    input_grad = total.astype(jnp.bfloat16).reshape(depth, chans_local, height, width)
    return (output_map, input_grad, kernel_grad)


def solution(mesh):
    return jax.shard_map(
        on_device,
        mesh=mesh,
        in_specs=(
            P("space", "chan", None, None),
            P(None, "chan", None),
            P("space", "chan", None, None),
        ),
        out_specs=(
            P("space", "chan", None, None),
            P("space", "chan", None, None),
            P(None, "chan", None),
        ),
        check_vma=False,
    )
```

profile of v0, /device:TPU:8, one launch (start us, length us, event | category | flops | bytes accessed | tf_op | source)
XLA Modules:
  0.0 456.1 jit_solution(4387820770311451748)
XLA Ops:
  7.2 0.8 fusion.80
  8.1 3.4 collective-permute-start.2
  11.5 1.3 collective-permute-start.3
  12.8 0.9 reshape.102
  13.7 3.6 collective-permute-done.3
  18.0 0.8 fusion.81
  18.9 4.7 %collective-permute-start = (bf16[1,16,1024]{2,1,0:T(8,128)(2,1)S(1)}, bf16[1,16,1024]{2,1,0:T(8,128)(2,1)S(1)}, u32[]{:S(2)}, u32[]{:S(2)}) collective-permute-start(bf16[1,16,1024]{2,1,0:T(8,128)(2,1)S(1)} %slice.120), channel_id=1, source_target_pairs={{0,16},{16,32},{32,48},{48,64},{64,80},{80,96},{96,112},{112,128},... | collective-permute-start | bytes 98312 | tf_op jit(solution)/shard_map/ppermute | solution.py:13
  23.6 1.3 collective-permute-start.1
  24.9 0.9 reshape.97
  25.8 3.6 collective-permute-done.1
  30.1 2.0 copy.40
  32.1 2.5 reshape.125
  34.6 7.4 %all-to-all-start = ((bf16[16,2,3456]{2,1,0:T(2,128)(2,1)}), bf16[16,2,3456]{2,1,0:T(2,128)(2,1)S(1)}, u32[]{:S(2)}, u32[]{:S(2)}) async-start(bf16[16,2,3456]{2,1,0:T(2,128)(2,1)} %reshape.125), calls=%async_computation | async-start | bytes 442368 | tf_op jit(solution)/shard_map/all_to_all | solution.py:45
  44.3 5.4 %all-to-all-done = bf16[16,2,3456]{2,1,0:T(2,128)(2,1)S(1)} async-done(((bf16[16,2,3456]{2,1,0:T(2,128)(2,1)}), bf16[16,2,3456]{2,1,0:T(2,128)(2,1)S(1)}, u32[]{:S(2)}, u32[]{:S(2)}) %all-to-all-start) | async-done | bytes 221216 | tf_op jit(solution)/shard_map/all_to_all | solution.py:45
  49.6 2.7 reshape.126
  52.3 4.2 copy.49
  57.0 0.8 copy.46
  58.4 0.8 copy.44
  59.9 0.8 copy.42
  61.3 26.4 %all-gather.5.cloned.1.call-done = bf16[4,256,1024]{2,1,0:T(8,128)(2,1)} async-done(((bf16[4,16,1024]{2,1,0:T(8,128)(2,1)}), bf16[4,256,1024]{2,1,0:T(8,128)(2,1)}) %all-gather.5.cloned.1.call-update) | async-done | bytes 2097168 | tf_op jit(solution)/shard_map/all_gather | solution.py:67
  87.7 3.8 fusion.29
  91.5 1.9 fusion.31
  93.3 2.6 fusion.33
  95.9 2.6 fusion.35
  98.5 1.9 multiply_dynamic-update-slice_fusion
  100.4 52.5 %all-gather.3.cloned.1.call-done = bf16[4,256,1024]{2,1,0:T(8,128)(2,1)} async-done(((bf16[4,16,1024]{2,1,0:T(8,128)(2,1)}), bf16[4,256,1024]{2,1,0:T(8,128)(2,1)}) %all-gather.3.cloned.1.call-update) | async-done | bytes 2097168 | tf_op jit(solution)/shard_map/all_gather | solution.py:49
  152.9 4.5 fusion.37
  157.3 2.7 fusion.39
  160.0 2.4 fusion.41
  162.4 1.3 fusion.17
  163.7 3.9 fusion.43
  168.3 1.2 fusion.21
  169.5 1.2 fusion.23
  171.3 1.1 fusion.27
  172.4 2.5 convolution_bitcast_fusion.2
  175.0 2.8 convolution_bitcast_fusion.1
  177.7 1.1 copy-done
  178.8 2.5 convolution_bitcast_fusion
  181.5 0.9 pad_maximum_fusion
  182.4 5.0 %fusion = f32[2,1024,16]{1,2,0:T(8,128)S(1)} fusion(bf16[16,2304,1]{1,0,2:T(8,128)(2,1)S(1)} %reshape.115, bf16[4,2304,1024]{2,1,0:T(8,128)(2,1)} %get-tuple-element.22), kind=kOutput, calls=%fused_computation | convolution fusion | flops 150994944 | bytes 9641984 | tf_op jit(solution)/shard_map/kj,zjp->zkp/dot_general | solution.py:74
  187.4 5.2 %fusion.2 = f32[2,1024,16]{1,2,0:T(8,128)S(1)} fusion(bf16[16,2304,1]{1,0,2:T(8,128)(2,1)S(1)} %reshape.114, bf16[4,2304,1024]{2,1,0:T(8,128)(2,1)} %get-tuple-element.22), kind=kOutput, calls=%fused_computation.2 | convolution fusion | flops 150994944 | bytes 9641984 | tf_op jit(solution)/shard_map/kj,zjp->zkp/dot_general | solution.py:74
  192.6 5.8 %fusion.56 = bf16[2,1024,16]{1,2,0:T(8,128)(2,1)S(1)} fusion(f32[2,1024,16]{1,2,0:T(8,128)S(1)} %fusion, f32[2,1024,16]{1,2,0:T(8,128)S(1)} %fusion.2, bf16[16,2304,1]{1,0,2:T(8,128)(2,1)S(1)} %reshape.113, bf16[4,2304,1024]{2,1,0:T(8,128)(2,1)} %get-tuple-element.22), kind=kOutput, calls=%fused_computation.69 | convolution fusion | flops 151093248 | bytes 9838592 | tf_op jit(solution)/shard_map/kj,zjp->zkp/dot_general | solution.py:74
  199.3 1.3 fusion.8
  200.6 1.3 fusion.6
  202.0 1.3 fusion.59
  204.0 243.3 %all-reduce.4.cloned.1.call-done = f32[27,16,256]{2,0,1:T(8,128)} async-done(((f32[27,16,256]{2,0,1:T(8,128)}), f32[27,16,256]{2,0,1:T(8,128)}) %all-reduce.4.cloned.1.call-update) | async-done | bytes 442384 | tf_op jit(solution)/shard_map/psum | solution.py:77
  447.3 1.1 broadcast_multiply_fusion
  448.4 1.0 copy.48
  (60 shorter events, 8.8 us)
Async XLA Ops:
  7.2 34.9 %copy-start.6 = (bf16[27,16,256]{2,1,0:T(8,128)(2,1)S(1)}, bf16[27,16,256]{2,1,0:T(8,128)(2,1)}, u32[]{:S(2)}) copy-start(bf16[27,16,256]{2,1,0:T(8,128)(2,1)} %param.4) | copy-start | bytes 663556
  7.2 80.5 %all-gather.5.cloned.1.call-start = ((), (), s32[]{:S(2)}) async-start(), calls=%async_computation.2 | async-start | bytes 2228224 | tf_op jit(solution)/shard_map/all_gather | solution.py:67
  8.1 5.6 %collective-permute-start.2 = (bf16[1,16,1024]{2,1,0:T(8,128)(2,1)S(1)}, bf16[1,16,1024]{2,1,0:T(8,128)(2,1)S(1)}, u32[]{:S(2)}, u32[]{:S(2)}) collective-permute-start(bf16[1,16,1024]{2,1,0:T(8,128)(2,1)S(1)} %slice.138), channel_id=1, source_target_pairs={{0,16},{16,32},{32,48},{48,64},{64,80},{80,96},{96,112},{112,128},... | collective-permute-start | bytes 98312 | tf_op jit(solution)/shard_map/ppermute | solution.py:13
  11.5 5.8 %collective-permute-start.3 = (bf16[1,16,1024]{2,1,0:T(8,128)(2,1)S(1)}, bf16[1,16,1024]{2,1,0:T(8,128)(2,1)S(1)}, u32[]{:S(2)}, u32[]{:S(2)}) collective-permute-start(bf16[1,16,1024]{2,1,0:T(8,128)(2,1)S(1)} %slice.140), channel_id=1, source_target_pairs={{16,0},{32,16},{48,32},{64,48},{80,64},{96,80},{112,96},{128,112},... | collective-permute-start | bytes 98312 | tf_op jit(solution)/shard_map/ppermute | solution.py:16
  13.7 16.4 %copy-start.4 = (bf16[2,16,1024]{2,1,0:T(8,128)(2,1)}, bf16[2,16,1024]{2,1,0:T(8,128)(2,1)S(1)}, u32[]{:S(2)}) copy-start(bf16[2,16,1024]{2,1,0:T(8,128)(2,1)S(1)} %reshape.102) | copy-start | bytes 196612
  18.0 134.9 %all-gather.3.cloned.1.call-start = ((), (), s32[]{:S(2)}) async-start(), calls=%async_computation.1 | async-start | bytes 2228224 | tf_op jit(solution)/shard_map/all_gather | solution.py:49
  18.9 6.9 %collective-permute-start = (bf16[1,16,1024]{2,1,0:T(8,128)(2,1)S(1)}, bf16[1,16,1024]{2,1,0:T(8,128)(2,1)S(1)}, u32[]{:S(2)}, u32[]{:S(2)}) collective-permute-start(bf16[1,16,1024]{2,1,0:T(8,128)(2,1)S(1)} %slice.120), channel_id=1, source_target_pairs={{0,16},{16,32},{32,48},{48,64},{64,80},{80,96},{96,112},{112,128},... | collective-permute-start | bytes 98312 | tf_op jit(solution)/shard_map/ppermute | solution.py:13
  23.6 5.8 %collective-permute-start.1 = (bf16[1,16,1024]{2,1,0:T(8,128)(2,1)S(1)}, bf16[1,16,1024]{2,1,0:T(8,128)(2,1)S(1)}, u32[]{:S(2)}, u32[]{:S(2)}) collective-permute-start(bf16[1,16,1024]{2,1,0:T(8,128)(2,1)S(1)} %slice.122), channel_id=1, source_target_pairs={{16,0},{32,16},{48,32},{64,48},{80,64},{96,80},{112,96},{128,112},... | collective-permute-start | bytes 98312 | tf_op jit(solution)/shard_map/ppermute | solution.py:16
  34.6 15.0 %all-to-all-start = ((bf16[16,2,3456]{2,1,0:T(2,128)(2,1)}), bf16[16,2,3456]{2,1,0:T(2,128)(2,1)S(1)}, u32[]{:S(2)}, u32[]{:S(2)}) async-start(bf16[16,2,3456]{2,1,0:T(2,128)(2,1)} %reshape.125), calls=%async_computation | async-start | bytes 442368 | tf_op jit(solution)/shard_map/all_to_all | solution.py:45
  42.0 405.2 %all-reduce.4.cloned.1.call-start = ((), (), s32[]{:S(2)}) async-start(), calls=%async_computation.3 | async-start | bytes 1048576 | tf_op jit(solution)/shard_map/psum | solution.py:77
  87.7 3.8 copy-start.2
  157.3 2.7 copy-start.3
  170.8 1.6 copy-start.5
  172.4 6.4 %copy-start = (bf16[4,2304,1024]{2,1,0:T(8,128)(2,1)}, bf16[4,2304,1024]{2,1,0:T(8,128)(2,1)S(1)}, u32[]{:S(2)}) copy-start(bf16[4,2304,1024]{2,1,0:T(8,128)(2,1)S(1)} %fusion.27) | copy-start | bytes 56623108
  187.4 11.8 %copy-start.1 = (bf16[4,2304,1024]{2,1,0:T(8,128)(2,1)S(1)}, bf16[4,2304,1024]{2,1,0:T(8,128)(2,1)}, u32[]{:S(2)}) copy-start(bf16[4,2304,1024]{2,1,0:T(8,128)(2,1)} %copy-done) | copy-start | bytes 56623108
  192.6 6.7 %copy-start.7 = (bf16[16,2304,1]{1,0,2:T(8,128)(2,1)S(1)}, bf16[16,2304,1]{1,0,2:T(8,128)(2,1)}, u32[]{:S(2)}) copy-start(bf16[16,2304,1]{1,0,2:T(8,128)(2,1)} %reshape.111) | copy-start | bytes 221188
  199.3 1.3 copy-start.8
  200.6 1.4 copy-start.9
Sparse Core Ops, SparseCore 0:
  18.1 69.4 all-gather.4
  91.1 61.7 all-gather.2
  182.5 264.7 all-reduce.3
where the time goes:
time: 462 us; the launch traced here: 456 us
  waiting for transfers between devices  335 us (73%)
  other arithmetic  35.5 us (8%)
  matrix products  27.8 us (6%)
  local copies, waits for them, and re-layouts  25.5 us (6%)
  starting transfers between devices  18.2 us (4%)
  between operations  14.3 us (3%)
    psum x1, waiting for transfers between devices, on_device(): kernel_grad = lax.psum(kernel_acc, 'space') * scale_factor  243 us
    all_gather x1, waiting for transfers between devices, on_device(): piece = lax.all_gather(rims, 'chan', axis=1, tiled=True)  52.5 us
    unnamed x13, other arithmetic  27.2 us
    all_gather x1, waiting for transfers between devices, on_device(): piece = lax.all_gather(grad_ext, 'chan', axis=1, tiled=True)  26.4 us
    dot_general x3, matrix products, on_device(): jnp.einsum('kj,zjp->zkp', weights, window, preferred_element_type=jnp.flo...  16 us
    unnamed x26, local copies, waits for them, and re-layouts  10.9 us
  transfers between devices with their start and end apart: 8, of which 6 were waited for; matrix products, arithmetic and copies ran while one was open for 12% of the time, Pallas kernels for 0%

commit v1 on v0

--- a/solution.py
+++ b/solution.py
@@ -74,7 +74,7 @@
         total = total + jnp.einsum(
             "kj,zjp->zkp", weights, window, preferred_element_type=jnp.float32
         )
-    kernel_grad = lax.psum(kernel_acc, "space") * scale_factor
+    kernel_grad = jnp.sum(lax.all_gather(kernel_acc, "space"), axis=0) * scale_factor
     output_map = output_acc.astype(jnp.bfloat16).reshape(depth, filters_local, height, width)
     input_grad = total.astype(jnp.bfloat16).reshape(depth, chans_local, height, width)
     return (output_map, input_grad, kernel_grad)

time: 462 us -> 532 us (1.15)
  the two profiles are of different devices: /device:TPU:8 before, /device:TPU:170 now
where the time goes in v1:
time: 532 us; the launch traced here: 523 us
  waiting for transfers between devices  383 us (72%)
  other arithmetic  52.8 us (10%)
  matrix products  31.2 us (6%)
  local copies, waits for them, and re-layouts  24.3 us (5%)
  starting transfers between devices  17.2 us (3%)
  between operations  14.5 us (3%)
    all_gather x1, waiting for transfers between devices, on_device(): lax.all_gather(kernel_acc, 'space')  266 us
    all_gather x1, waiting for transfers between devices, on_device(): piece = lax.all_gather(grad_ext, 'chan', axis=1, tiled=True)  53.4 us
    all_gather x1, waiting for transfers between devices, on_device(): piece = lax.all_gather(rims, 'chan', axis=1, tiled=True)  52.6 us
    unnamed x14, other arithmetic  26.9 us
    concatenate x2, other arithmetic, plane_stack(): return jnp.concatenate(windows, axis=1)  17 us
    dot_general x3, matrix products, on_device(): jnp.einsum('kj,zjp->zkp', weights, window, preferred_element_type=jnp.flo...  15.6 us
  transfers between devices with their start and end apart: 8, of which 6 were waited for; matrix products, arithmetic and copies ran while one was open for 11% of the time, Pallas kernels for 0%

profile of v1, /device:TPU:170, one launch (start us, length us, event | category | flops | bytes accessed | tf_op | source)
XLA Modules:
  0.0 522.7 jit_solution(12112781176393899376)
XLA Ops:
  7.2 0.8 fusion.80
  8.0 3.8 collective-permute-start.2
  11.8 2.0 collective-permute-start.3
  13.9 0.9 reshape.102
  14.8 3.8 collective-permute-done.3
  19.3 0.8 fusion.81
  20.1 2.5 collective-permute-start
  22.6 3.3 collective-permute-start.1
  26.0 0.9 reshape.97
  26.9 2.5 collective-permute-done.1
  30.1 53.4 %all-gather.7.cloned.1.call-done = bf16[4,256,1024]{2,1,0:T(8,128)(2,1)} async-done(((bf16[4,16,1024]{2,1,0:T(8,128)(2,1)}), bf16[4,256,1024]{2,1,0:T(8,128)(2,1)}) %all-gather.7.cloned.1.call-update) | async-done | bytes 2097168 | tf_op jit(solution)/shard_map/all_gather | solution.py:67
  83.5 3.8 fusion.29
  87.3 1.9 fusion.31
  89.2 2.6 fusion.33
  91.8 2.5 fusion.35
  94.3 1.9 multiply_dynamic-update-slice_fusion
  96.2 52.6 %all-gather.5.cloned.1.call-done = bf16[4,256,1024]{2,1,0:T(8,128)(2,1)} async-done(((bf16[4,16,1024]{2,1,0:T(8,128)(2,1)}), bf16[4,256,1024]{2,1,0:T(8,128)(2,1)}) %all-gather.5.cloned.1.call-update) | async-done | bytes 2097168 | tf_op jit(solution)/shard_map/all_gather | solution.py:49
  148.7 4.5 fusion.37
  153.2 2.7 fusion.39
  155.9 2.2 fusion.41
  158.1 1.3 fusion.17
  159.4 15.9 %fusion.43 = (bf16[4,2304,1024]{2,1,0:T(8,128)(2,1)}, bf16[4,2304,1024]{2,1,0:T(8,128)(2,1)S(1)}) fusion(bf16[4,2304,1024]{2,1,0:T(8,128)(2,1)} %get-tuple-element.15, bf16[4,256,1024]{2,1,0:T(8,128)(2,1)S(1)} %copy-done.1, bf16[1024]{0:T(1024)(128)(2,1)S(1)} %fusion.75, bf16[4,2304,1024]{2,1,0:T(8,128)(2,1)S(1)} %fusion.17, ...), kind=kLoop, calls=%fused_computation.62 | loop fusion | flops 7340032 | bytes 8390656 | tf_op jit(solution)/shard_map/concatenate | solution.py:35
  176.0 1.2 fusion.21
  177.2 1.2 fusion.23
  179.0 1.1 fusion.27
  180.1 2.5 convolution_bitcast_fusion.2
  182.6 2.6 convolution_bitcast_fusion.1
  185.2 1.3 copy-done
  186.5 2.5 convolution_bitcast_fusion
  189.2 1.0 copy.45
  190.3 1.1 copy.37
  191.4 2.5 reshape.126
  193.9 5.4 %all-to-all-start = ((bf16[16,2,3456]{2,1,0:T(2,128)(2,1)}), bf16[16,2,3456]{2,1,0:T(2,128)(2,1)S(1)}, u32[]{:S(2)}, u32[]{:S(2)}) async-start(bf16[16,2,3456]{2,1,0:T(2,128)(2,1)} %reshape.126), calls=%async_computation | async-start | bytes 442368 | tf_op jit(solution)/shard_map/all_to_all | solution.py:45
  201.5 4.4 all-to-all-done
  205.9 2.7 reshape.127
  208.6 3.9 copy.46
  213.0 0.8 copy.43
  214.4 0.8 copy.41
  215.8 0.8 copy.39
  217.3 5.2 fusion
  222.5 5.2 fusion.2
  227.7 5.2 fusion.56
  233.6 5.2 fusion.8
  238.9 1.3 fusion.6
  240.2 1.4 fusion.59
  242.2 266.1 %all-gather.9.cloned.1.call-done = f32[864,16,256]{2,1,0:T(8,128)} async-done(((f32[27,16,256]{2,1,0:T(8,128)}), f32[864,16,256]{2,1,0:T(8,128)}) %all-gather.9.cloned.1.call-update) | async-done | bytes 14155792 | tf_op jit(solution)/shard_map/all_gather | solution.py:77
  508.3 6.7 %reduce_sum.9 = f32[27,16,256]{2,1,0:T(8,128)S(1)} reduce(f32[32,27,16,256]{3,2,1,0:T(8,128)} %bitcast.77, f32[]{:T(128)} %constant.30.clone.1), dimensions={0}, to_apply=%region_0.1 | reduce | flops 3428352 | bytes 14598148 | tf_op jit(solution)/shard_map/reduce_sum | solution.py:77
  515.0 0.8 broadcast_multiply_fusion
  (66 shorter events, 8.7 us)
Async XLA Ops:
  7.2 76.4 %all-gather.7.cloned.1.call-start = ((), (), s32[]{:S(2)}) async-start(), calls=%async_computation.2 | async-start | bytes 2228224 | tf_op jit(solution)/shard_map/all_gather | solution.py:67
  8.0 6.8 %collective-permute-start.2 = (bf16[1,16,1024]{2,1,0:T(8,128)(2,1)S(1)}, bf16[1,16,1024]{2,1,0:T(8,128)(2,1)S(1)}, u32[]{:S(2)}, u32[]{:S(2)}) collective-permute-start(bf16[1,16,1024]{2,1,0:T(8,128)(2,1)S(1)} %slice.138), channel_id=1, source_target_pairs={{0,16},{16,32},{32,48},{48,64},{64,80},{80,96},{96,112},{112,128},... | collective-permute-start | bytes 98312 | tf_op jit(solution)/shard_map/ppermute | solution.py:13
  11.8 6.7 %collective-permute-start.3 = (bf16[1,16,1024]{2,1,0:T(8,128)(2,1)S(1)}, bf16[1,16,1024]{2,1,0:T(8,128)(2,1)S(1)}, u32[]{:S(2)}, u32[]{:S(2)}) collective-permute-start(bf16[1,16,1024]{2,1,0:T(8,128)(2,1)S(1)} %slice.140), channel_id=1, source_target_pairs={{16,0},{32,16},{48,32},{64,48},{80,64},{96,80},{112,96},{128,112},... | collective-permute-start | bytes 98312 | tf_op jit(solution)/shard_map/ppermute | solution.py:16
  19.3 129.5 %all-gather.5.cloned.1.call-start = ((), (), s32[]{:S(2)}) async-start(), calls=%async_computation.1 | async-start | bytes 2228224 | tf_op jit(solution)/shard_map/all_gather | solution.py:49
  20.1 6.8 %collective-permute-start = (bf16[1,16,1024]{2,1,0:T(8,128)(2,1)S(1)}, bf16[1,16,1024]{2,1,0:T(8,128)(2,1)S(1)}, u32[]{:S(2)}, u32[]{:S(2)}) collective-permute-start(bf16[1,16,1024]{2,1,0:T(8,128)(2,1)S(1)} %slice.120), channel_id=1, source_target_pairs={{0,16},{16,32},{32,48},{48,64},{64,80},{80,96},{96,112},{112,128},... | collective-permute-start | bytes 98312 | tf_op jit(solution)/shard_map/ppermute | solution.py:13
  22.6 6.7 %collective-permute-start.1 = (bf16[1,16,1024]{2,1,0:T(8,128)(2,1)S(1)}, bf16[1,16,1024]{2,1,0:T(8,128)(2,1)S(1)}, u32[]{:S(2)}, u32[]{:S(2)}) collective-permute-start(bf16[1,16,1024]{2,1,0:T(8,128)(2,1)S(1)} %slice.122), channel_id=1, source_target_pairs={{16,0},{32,16},{48,32},{64,48},{80,64},{96,80},{112,96},{128,112},... | collective-permute-start | bytes 98312 | tf_op jit(solution)/shard_map/ppermute | solution.py:16
  30.0 478.3 %all-gather.9.cloned.1.call-start = ((), (), s32[]{:S(2)}) async-start(), calls=%async_computation.3 | async-start | bytes 14598144 | tf_op jit(solution)/shard_map/all_gather | solution.py:77
  83.5 3.8 copy-start.1
  153.2 2.7 copy-start.2
  180.1 6.4 %copy-start = (bf16[4,2304,1024]{2,1,0:T(8,128)(2,1)}, bf16[4,2304,1024]{2,1,0:T(8,128)(2,1)S(1)}, u32[]{:S(2)}) copy-start(bf16[4,2304,1024]{2,1,0:T(8,128)(2,1)S(1)} %fusion.27) | copy-start | bytes 56623108
  186.5 3.8 copy-start.3
  193.9 12.0 %all-to-all-start = ((bf16[16,2,3456]{2,1,0:T(2,128)(2,1)}), bf16[16,2,3456]{2,1,0:T(2,128)(2,1)S(1)}, u32[]{:S(2)}, u32[]{:S(2)}) async-start(bf16[16,2,3456]{2,1,0:T(2,128)(2,1)} %reshape.126), calls=%async_computation | async-start | bytes 442368 | tf_op jit(solution)/shard_map/all_to_all | solution.py:45
  217.3 21.6 %slice-start = ((s8[18874368]{0:T(1024)(128)(4,1)}), s8[4194304]{0:T(1024)(128)(4,1)S(1)}, s32[]{:S(2)}) async-start(s8[18874368]{0:T(1024)(128)(4,1)} %bitcast.75), calls=%async_computation.4 | async-start | bytes 8388608
  217.3 21.5 %slice-start.1 = ((s8[18874368]{0:T(1024)(128)(4,1)}), s8[4194304]{0:T(1024)(128)(4,1)S(1)}, s32[]{:S(2)}) async-start(s8[18874368]{0:T(1024)(128)(4,1)} %bitcast.75), calls=%async_computation.5 | async-start | bytes 8388608
  222.5 16.3 %slice-start.2 = ((s8[18874368]{0:T(1024)(128)(4,1)}), s8[4194304]{0:T(1024)(128)(4,1)S(1)}, s32[]{:S(2)}) async-start(s8[18874368]{0:T(1024)(128)(4,1)} %bitcast.75), calls=%async_computation.6 | async-start | bytes 8388608
  227.7 5.9 %copy-start.4 = (bf16[16,2304,1]{1,0,2:T(8,128)(2,1)S(1)}, bf16[16,2304,1]{1,0,2:T(8,128)(2,1)}, u32[]{:S(2)}) copy-start(bf16[16,2304,1]{1,0,2:T(8,128)(2,1)} %reshape.112) | copy-start | bytes 221188
  227.7 11.1 %slice-start.3 = ((s8[18874368]{0:T(1024)(128)(4,1)}), s8[4194304]{0:T(1024)(128)(4,1)S(1)}, s32[]{:S(2)}) async-start(s8[18874368]{0:T(1024)(128)(4,1)} %bitcast.75), calls=%async_computation.7 | async-start | bytes 8388608
  233.6 5.3 %slice-start.4 = ((s8[18874368]{0:T(1024)(128)(4,1)}), s8[2097152]{0:T(1024)(128)(4,1)S(1)}, s32[]{:S(2)}) async-start(s8[18874368]{0:T(1024)(128)(4,1)} %bitcast.75), calls=%async_computation.8 | async-start | bytes 4194304
  233.6 5.3 %copy-start.5 = (bf16[16,2304,1]{1,0,2:T(8,128)(2,1)S(1)}, bf16[16,2304,1]{1,0,2:T(8,128)(2,1)}, u32[]{:S(2)}) copy-start(bf16[16,2304,1]{1,0,2:T(8,128)(2,1)} %reshape.113) | copy-start | bytes 221188
  238.9 1.3 copy-start.6
Sparse Core Ops, SparseCore 0:
  19.4 64.1 all-gather.6
  86.9 61.7 all-gather.4
  190.4 317.8 all-gather.8
